TPU v7x, 512 devices: a whole 4x4x16 slice. The times are simulated.
512 devices in a mesh: expert: 32 (over z, core), tensor: 16 (over y, x).
Axes of the slice: x: 4, y: 4, z: 16, core: 2. Of those that a mesh axis runs over, the one named last changes fastest.
Arguments:
- hidden_in: bfloat16 [4096, 4096], P('expert', 'tensor'), may hold values from -92 to 92
- norm_gain: float32 [4096], P('tensor'), may hold values from 0.5 to 1.5
- expert_ids: int32 [4096, 8], P('expert'), may hold values from 0 to 63, all different within a row; in each aligned block of 128 rows (0 to 127, 128 to 255, ...) at most 24 rows name the same one
- route_weights: float32 [4096, 8], P('expert'), may hold values from 0.05 to 0.5
- w_gate: bfloat16 [64, 1536, 4096], P('expert', 'tensor'), may hold values from -0.09375 to 0.09375
- w_up: bfloat16 [64, 1536, 4096], P('expert', 'tensor'), may hold values from -0.09375 to 0.09375
- w_down: bfloat16 [64, 1536, 4096], P('expert', 'tensor'), may hold values from -0.15625 to 0.15625
Outputs:
- moe_out: bfloat16 [4096, 4096], P('expert', 'tensor')
Inputs may be any that keep to these rules, and one draw needn't show every extreme that they name: `expert_ids`: in each aligned block of 128 rows (the rows of one index of the expert axis) no expert is named by more than 24 rows, a bound that some block reaches.
All inputs are finite; a program needn't handle non-finite values.
Results may differ from a plain program's by a relative error of at most 0.019.
Values may be sent and summed in bfloat16 or wider, within the bound.
A program may use at most 128 MiB of HBM per device.

v0:
```python
import jax
import jax.numpy as jnp
from jax import lax
from jax.sharding import PartitionSpec as P

D = 4096
epsilon = 1e-06


def body(hidden_in, norm_gain, expert_ids, route_weights, w_gate, w_up, w_down):
    tokens_here = hidden_in.shape[0]
    choices_count = expert_ids.shape[1]
    exp_local = w_gate.shape[0]
    groups = lax.axis_size("expert")
    experts_all = exp_local * groups
    capacity = min(tokens_here, 3 * tokens_here * choices_count // (2 * experts_all))
    widened = hidden_in.astype(jnp.float32)
    squares = lax.psum(jnp.sum(widened * widened, axis=1), "tensor")
    normed = (widened * lax.rsqrt(squares / D + epsilon)[:, None] * norm_gain[None, :]).astype(
        jnp.bfloat16
    )
    routing = jnp.concatenate([expert_ids.astype(jnp.float32), route_weights], axis=1)
    routing = lax.all_gather(routing.T, "expert", axis=0, tiled=False)
    tokens_all = lax.all_gather(normed, "expert", axis=0, tiled=False)
    first = (lax.axis_index("expert") * exp_local).astype(jnp.float32)
    named = (
        routing[:, None, :choices_count, :]
        == first + jnp.arange(exp_local, dtype=jnp.float32)[None, :, None, None]
    )
    chosen = jnp.any(named, axis=2)
    scale = jnp.sum(jnp.where(named, routing[:, None, choices_count:, :], 0.0), axis=2)
    step = jnp.arange(tokens_here, dtype=jnp.int32)
    earlier = (step[:, None] < step[None, :]).astype(jnp.bfloat16)
    position = jnp.einsum(
        "bjs,st->bjt", chosen.astype(jnp.bfloat16), earlier, preferred_element_type=jnp.float32
    )
    slot = jnp.arange(capacity, dtype=jnp.float32)
    select = (
        (position[:, :, None, :] == slot[None, None, :, None]) & chosen[:, :, None, :]
    ).astype(jnp.bfloat16)
    rows = jnp.einsum(
        "bjst,btd->bjsd", select, tokens_all, preferred_element_type=jnp.float32
    ).astype(jnp.bfloat16)
    rows = rows.transpose(1, 0, 2, 3).reshape(exp_local, groups * capacity, -1)
    piece = lax.all_gather(rows, "tensor", axis=2, tiled=True)
    gate_add = jnp.einsum("erd,efd->erf", piece, w_gate, preferred_element_type=jnp.float32)
    up_add = jnp.einsum("erd,efd->erf", piece, w_up, preferred_element_type=jnp.float32)
    inner = (jax.nn.silu(gate_add) * up_add).astype(jnp.bfloat16)
    partials = jnp.einsum("erf,efd->erd", inner, w_down, preferred_element_type=jnp.float32).astype(
        jnp.bfloat16
    )
    summed = lax.psum_scatter(partials, "tensor", scatter_dimension=2, tiled=True)
    summed = summed.reshape(exp_local, groups, capacity, -1)
    back = jnp.einsum("bjst,jbsd->bjtd", select, summed, preferred_element_type=jnp.float32)
    weighted = jnp.sum(back * scale[:, :, :, None], axis=1).astype(jnp.bfloat16)
    return lax.psum_scatter(weighted, "expert", scatter_dimension=0, tiled=False)


def solution(mesh):
    placed = (
        P("expert", "tensor"),
        P("tensor"),
        P("expert", None),
        P("expert", None),
        P("expert", "tensor", None),
        P("expert", "tensor", None),
        P("expert", "tensor", None),
    )
    return jax.shard_map(
        body, mesh=mesh, in_specs=placed, out_specs=P("expert", "tensor"), check_vma=False
    )
```

profile of v0, /device:TPU:18, one launch (start us, length us, event | category | flops | bytes accessed | tf_op | source)
XLA Modules:
  0.0 491.3 jit_solution(8719006843433217021)
XLA Ops:
  6.5 0.0 copy-start
  6.5 0.0 all-gather.7.cloned.1.call-start
  6.5 1.1 fusion.17
  7.6 31.1 %psum.7 = f32[128]{0:T(128)S(1)} all-reduce(f32[128]{0:T(128)S(1)} %fusion.17), channel_id=1, replica_groups=mesh['expert'=32,'tensor'=16] {'tensor'}, use_global_device_ids=true, to_apply=%region_2.0 | all-reduce | flops 128 | bytes 1024 | tf_op jit(solution)/shard_map/psum | solution.py:18
  38.8 1.6 fusion.19
  40.3 0.0 all-gather.7.cloned.1.call-update
  40.3 0.0 all-gather.5.cloned.1.call-start
  40.4 0.7 convert_element_type.31
  41.1 0.7 maximum_bitcast_fusion
  41.8 37.0 %all-gather = f32[512,128]{1,0:T(8,128)S(1)} all-gather(f32[16,128]{1,0:T(8,128)S(1)} %maximum_bitcast_fusion), channel_id=2, replica_groups=mesh['expert'=32,'tensor'=16] {'expert'}, dimensions={0}, use_global_device_ids=true | all-gather | bytes 270336 | tf_op jit(solution)/shard_map/all_gather | solution.py:23
  78.8 0.2 compare_reduce_fusion
  79.0 0.1 fusion.21
  79.2 41.8 %all-gather.7.cloned.1.call-done = bf16[4096,256]{1,0:T(8,128)(2,1)} async-done(((bf16[128,256]{1,0:T(8,128)(2,1)}), bf16[4096,256]{1,0:T(8,128)(2,1)}) %all-gather.7.cloned.1.call-update) | async-done | bytes 2097168 | tf_op jit(solution)/shard_map/all_gather | solution.py:24
  121.0 2.0 fusion
  123.0 1.0 copy.17
  124.0 0.0 all-gather.5.cloned.1.call-update
  124.0 0.0 reduce-scatter.3.cloned.1.call-start
  124.1 110.4 %all-gather.5.cloned.1.call-done = bf16[2,768,4096]{2,1,0:T(8,128)(2,1)} async-done(((bf16[2,768,256]{2,1,0:T(8,128)(2,1)}), bf16[2,768,4096]{2,1,0:T(8,128)(2,1)}) %all-gather.5.cloned.1.call-update) | async-done | bytes 12582928 | tf_op jit(solution)/shard_map/all_gather | solution.py:45
  234.4 9.0 %fusion.26 = f32[2,768,96]{1,2,0:T(8,128)S(1)} fusion(bf16[2,768,4096]{2,1,0:T(8,128)(2,1)} %all-gather.5.cloned.1.call-done, bf16[2,96,4096]{2,1,0:T(8,128)(2,1)} %param.11), kind=kOutput, calls=%fused_computation.36 | convolution fusion | flops 1207959552 | bytes 14745600 | tf_op jit(solution)/shard_map/erd,efd->erf/dot_general | solution.py:46
  243.4 0.0 copy-done
  243.4 15.3 %convolution_convert_fusion = bf16[2,768,4096]{2,1,0:T(8,128)(2,1)} fusion(bf16[2,96,4096]{2,1,0:T(8,128)(2,1)S(1)} %copy-done, bf16[2,768,4096]{2,1,0:T(8,128)(2,1)} %all-gather.5.cloned.1.call-done, bf16[2,96,4096]{2,1,0:T(8,128)(2,1)} %param.12, f32[2,768,96]{1,2,0:T(8,128)S(1)} %fusion.26), kind=kOutput, calls=%fused_computation | convolution fusion | flops 2423095296 | bytes 28901376 | tf_op jit(solution)/shard_map/erf,efd->erd/dot_general | solution.py:49
  258.7 0.0 reduce-scatter.3.cloned.1.call-update
  258.8 0.0 reduce-scatter.5.cloned.1.call-start
  258.8 0.2 fusion.16
  259.0 109.0 %reduce-scatter.3.cloned.1.call-done = bf16[2,768,256]{2,1,0:T(8,128)(2,1)} async-done(((bf16[2,768,4096]{2,1,0:T(8,128)(2,1)}), bf16[2,768,256]{2,1,0:T(8,128)(2,1)}) %reduce-scatter.3.cloned.1.call-update) | async-done | bytes 786448 | tf_op jit(solution)/shard_map/reduce_scatter | solution.py:52
  368.0 5.3 %multiply_reduce_fusion = bf16[32,128,256]{2,1,0:T(8,128)(2,1)} fusion(f32[32,2,128]{2,1,0:T(2,128)S(1)} %fusion.16, bf16[2,32,24,256]{3,2,1,0:T(8,128)(2,1)} %bitcast.25, f32[32,2,128]{2,1,0:T(2,128)S(1)} %copy.16, pred[32,2,128]{2,1,0:T(4,128)(4,1)S(1)} %compare_reduce_fusion), kind=kOutput, calls=%fused_computation.1 | convolution fusion | flops 104202240 | bytes 2957312 | tf_op jit(solution)/shard_map/bjst,jbsd->bjtd/dot_general | solution.py:54
  373.3 0.0 reduce-scatter.5.cloned.1.call-update
  373.3 111.5 %reduce-scatter.5.cloned.1.call-done = bf16[1,128,256]{2,1,0:T(8,128)(2,1)} async-done(((bf16[32,128,256]{2,1,0:T(8,128)(2,1)}), bf16[1,128,256]{2,1,0:T(8,128)(2,1)}) %reduce-scatter.5.cloned.1.call-update) | async-done | bytes 65552 | tf_op jit(solution)/shard_map/reduce_scatter | solution.py:56
  (4 shorter events, 0.1 us)
Async XLA Ops:
  6.5 236.9 %copy-start = (bf16[2,96,4096]{2,1,0:T(8,128)(2,1)S(1)}, bf16[2,96,4096]{2,1,0:T(8,128)(2,1)}, u32[]{:S(2)}) copy-start(bf16[2,96,4096]{2,1,0:T(8,128)(2,1)} %param.13) | copy-start | bytes 4718596
  6.5 114.5 %all-gather.7.cloned.1.call-start = ((), (), s32[]{:S(2)}) async-start(), calls=%async_computation.5 | async-start | bytes 2162688 | tf_op jit(solution)/shard_map/all_gather | solution.py:24
  40.3 194.1 %all-gather.5.cloned.1.call-start = ((), (), s32[]{:S(2)}) async-start(), calls=%async_computation.2 | async-start | bytes 13369344 | tf_op jit(solution)/shard_map/all_gather | solution.py:45
  124.0 243.9 %reduce-scatter.3.cloned.1.call-start = ((), (), s32[]{:S(2)}) async-start(), calls=%async_computation.3 | async-start | bytes 13369344 | tf_op jit(solution)/shard_map/reduce_scatter | solution.py:52
  258.8 226.0 %reduce-scatter.5.cloned.1.call-start = ((), (), s32[]{:S(2)}) async-start(), calls=%async_computation.4 | async-start | bytes 2162688 | tf_op jit(solution)/shard_map/reduce_scatter | solution.py:56
Sparse Core Ops, SparseCore 0:
  40.5 80.4 all-gather.6
  124.1 110.2 all-gather.4
  258.9 109.0 reduce-scatter.2
  373.4 111.3 reduce-scatter.4
where the time goes:
time: 492 us; the launch traced here: 491 us
  waiting for transfers between devices  373 us (76%)
  blocking collectives  68.2 us (14%)
  matrix products  31.7 us (6%)
  between operations  13.2 us (3%)
    reduce_scatter x1, waiting for transfers between devices, body(): lax.psum_scatter(weighted, 'expert', scatter_dimension=0, tiled=False)  111 us
    all_gather x1, waiting for transfers between devices, body(): piece = lax.all_gather(rows, 'tensor', axis=2, tiled=True)  110 us
    reduce_scatter x1, waiting for transfers between devices, body(): lax.psum_scatter(partials, 'tensor', scatter_dimension=2, tiled=True)  109 us
    all_gather x1, waiting for transfers between devices, body(): tokens_all = lax.all_gather(normed, 'expert', axis=0, tiled=False)  41.8 us
    all_gather x1, blocking collectives, body(): routing = lax.all_gather(routing.T, 'expert', axis=0, tiled=False)  37 us
    psum x1, blocking collectives, body(): squares = lax.psum(jnp.sum(widened * widened, axis=1), 'tensor')  31.1 us
    dot_general x1, matrix products, body(): jnp.einsum('erf,efd->erd', inner, w_down, preferred_element_type=jnp.floa...  15.3 us
  transfers between devices with their start and end apart: 4, of which 4 were waited for; matrix products, arithmetic and copies ran while one was open for 0% of the time, Pallas kernels for 0%

commit v1 on v0

--- a/solution.py
+++ b/solution.py
@@ -5,6 +5,14 @@
 
 D = 4096
 epsilon = 1e-06
+
+
+def gather_by_exchange(array, axis, dim):
+    size = lax.axis_size(axis)
+    repeats = [size if d == dim else 1 for d in range(array.ndim)]
+    return lax.all_to_all(
+        jnp.tile(array, repeats), axis, split_axis=dim, concat_axis=dim, tiled=True
+    )
 
 
 def body(hidden_in, norm_gain, expert_ids, route_weights, w_gate, w_up, w_down):
@@ -42,7 +50,7 @@
         "bjst,btd->bjsd", select, tokens_all, preferred_element_type=jnp.float32
     ).astype(jnp.bfloat16)
     rows = rows.transpose(1, 0, 2, 3).reshape(exp_local, groups * capacity, -1)
-    piece = lax.all_gather(rows, "tensor", axis=2, tiled=True)
+    piece = gather_by_exchange(rows, "tensor", 2)
     gate_add = jnp.einsum("erd,efd->erf", piece, w_gate, preferred_element_type=jnp.float32)
     up_add = jnp.einsum("erd,efd->erf", piece, w_up, preferred_element_type=jnp.float32)
     inner = (jax.nn.silu(gate_add) * up_add).astype(jnp.bfloat16)

time: 492 us -> 564 us (1.15)
  the two profiles are of different devices: /device:TPU:18 before, /device:TPU:2 now
where the time goes in v1:
time: 564 us; the launch traced here: 563 us
  waiting for transfers between devices  250 us (44%)
  blocking collectives  221 us (39%)
  local copies, waits for them, and re-layouts  42.9 us (8%)
  matrix products  31.7 us (6%)
  between operations  13.2 us (2%)
    all_to_all x1, blocking collectives, gather_by_exchange(): lax.all_to_all(jnp.tile(array, repeats), axis, split_axis=dim, concat_axi...  147 us
    reduce_scatter x1, waiting for transfers between devices, body(): lax.psum_scatter(weighted, 'expert', scatter_dimension=0, tiled=False)  110 us
    reduce_scatter x1, waiting for transfers between devices, body(): lax.psum_scatter(partials, 'tensor', scatter_dimension=2, tiled=True)  103 us
    psum x1, blocking collectives, body(): squares = lax.psum(jnp.sum(widened * widened, axis=1), 'tensor')  41.4 us
    all_gather x1, waiting for transfers between devices, body(): tokens_all = lax.all_gather(normed, 'expert', axis=0, tiled=False)  36.6 us
    all_gather x1, blocking collectives, body(): routing = lax.all_gather(routing.T, 'expert', axis=0, tiled=False)  32.2 us
    all_to_all x1, local copies, waits for them, and re-layouts, gather_by_exchange(): lax.all_to_all(jnp.tile(array, repeats), axis, split_axis=dim, concat_axi...  31.1 us
    dot_general x1, matrix products, body(): jnp.einsum('erf,efd->erd', inner, w_down, preferred_element_type=jnp.floa...  15.3 us
  transfers between devices with their start and end apart: 3, of which 3 were waited for; matrix products, arithmetic and copies ran while one was open for 0% of the time, Pallas kernels for 0%

profile of v1, /device:TPU:2, one launch (start us, length us, event | category | flops | bytes accessed | tf_op | source)
XLA Modules:
  0.0 562.8 jit_solution(14428305000905469262)
XLA Ops:
  6.5 0.0 copy-start
  6.5 0.0 all-gather.4.cloned.1.call-start
  6.5 1.1 fusion.17
  7.6 41.4 %psum.7 = f32[128]{0:T(128)S(1)} all-reduce(f32[128]{0:T(128)S(1)} %fusion.17), channel_id=1, replica_groups=mesh['expert'=32,'tensor'=16] {'tensor'}, use_global_device_ids=true, to_apply=%region_2.0 | all-reduce | flops 128 | bytes 1024 | tf_op jit(solution)/shard_map/psum | solution.py:26
  49.0 1.6 fusion.19
  50.5 0.0 all-gather.4.cloned.1.call-update
  50.6 0.0 reduce-scatter.3.cloned.1.call-start
  50.6 0.7 convert_element_type.31
  51.3 0.7 maximum_bitcast_fusion
  52.0 32.2 %all-gather = f32[512,128]{1,0:T(8,128)S(1)} all-gather(f32[16,128]{1,0:T(8,128)S(1)} %maximum_bitcast_fusion), channel_id=2, replica_groups=mesh['expert'=32,'tensor'=16] {'expert'}, dimensions={0}, use_global_device_ids=true | all-gather | bytes 270336 | tf_op jit(solution)/shard_map/all_gather | solution.py:31
  84.3 0.2 compare_reduce_fusion
  84.4 0.1 fusion.21
  84.6 36.6 %all-gather.4.cloned.1.call-done = bf16[4096,256]{1,0:T(8,128)(2,1)} async-done(((bf16[128,256]{1,0:T(8,128)(2,1)}), bf16[4096,256]{1,0:T(8,128)(2,1)}) %all-gather.4.cloned.1.call-update) | async-done | bytes 2097168 | tf_op jit(solution)/shard_map/all_gather | solution.py:32
  121.2 2.0 fusion
  123.2 0.1 copy.24
  123.3 0.8 copy.25
  124.1 10.9 %tile.11 = bf16[2,768,16,256]{1,0,3,2:T(2,128)(2,1)S(1)} broadcast(bf16[2,768,256]{1,0,2:T(2,128)(2,1)S(1)} %copy.25), dimensions={0,1,3} | broadcast | bytes 13369344 | tf_op jit(solution)/shard_map/tile | solution.py:14
  135.0 146.9 %all_to_all.5 = bf16[2,768,4096]{1,0,2:T(2,128)(2,1)} all-to-all(bf16[2,768,4096]{1,0,2:T(2,128)(2,1)S(1)} %bitcast.23), channel_id=1, replica_groups=mesh['expert'=32,'tensor'=16] {'tensor'}, dimensions={2} | all-to-all | bytes 25165824 | tf_op jit(solution)/shard_map/all_to_all | solution.py:13
  281.9 31.1 %copy.26 = bf16[2,768,4096]{2,1,0:T(8,128)(2,1)} copy(bf16[2,768,4096]{1,0,2:T(2,128)(2,1)} %all_to_all.5) | data formatting | bytes 25165824 | tf_op jit(solution)/shard_map/all_to_all | solution.py:13
  313.0 9.0 %fusion.26 = f32[2,768,96]{1,2,0:T(8,128)S(1)} fusion(bf16[2,768,4096]{2,1,0:T(8,128)(2,1)} %copy.26, bf16[2,96,4096]{2,1,0:T(8,128)(2,1)} %param.11), kind=kOutput, calls=%fused_computation.36 | convolution fusion | flops 1207959552 | bytes 14745600 | tf_op jit(solution)/shard_map/erd,efd->erf/dot_general | solution.py:54
  322.0 0.0 copy-done
  322.0 15.3 %convolution_convert_fusion = bf16[2,768,4096]{2,1,0:T(8,128)(2,1)} fusion(bf16[2,96,4096]{2,1,0:T(8,128)(2,1)S(1)} %copy-done, bf16[2,768,4096]{2,1,0:T(8,128)(2,1)} %copy.26, bf16[2,96,4096]{2,1,0:T(8,128)(2,1)} %param.12, f32[2,768,96]{1,2,0:T(8,128)S(1)} %fusion.26), kind=kOutput, calls=%fused_computation | convolution fusion | flops 2423095296 | bytes 28901376 | tf_op jit(solution)/shard_map/erf,efd->erd/dot_general | solution.py:57
  337.3 0.0 reduce-scatter.3.cloned.1.call-update
  337.3 0.0 reduce-scatter.5.cloned.1.call-start
  337.4 0.2 fusion.16
  337.6 103.4 %reduce-scatter.3.cloned.1.call-done = bf16[2,768,256]{2,1,0:T(8,128)(2,1)} async-done(((bf16[2,768,4096]{2,1,0:T(8,128)(2,1)}), bf16[2,768,256]{2,1,0:T(8,128)(2,1)}) %reduce-scatter.3.cloned.1.call-update) | async-done | bytes 786448 | tf_op jit(solution)/shard_map/reduce_scatter | solution.py:60
  440.9 5.3 multiply_reduce_fusion
  446.2 0.0 reduce-scatter.5.cloned.1.call-update
  446.3 110.0 %reduce-scatter.5.cloned.1.call-done = bf16[1,128,256]{2,1,0:T(8,128)(2,1)} async-done(((bf16[32,128,256]{2,1,0:T(8,128)(2,1)}), bf16[1,128,256]{2,1,0:T(8,128)(2,1)}) %reduce-scatter.5.cloned.1.call-update) | async-done | bytes 65552 | tf_op jit(solution)/shard_map/reduce_scatter | solution.py:64
  (4 shorter events, 0.1 us)
Async XLA Ops:
  6.5 315.4 %copy-start = (bf16[2,96,4096]{2,1,0:T(8,128)(2,1)S(1)}, bf16[2,96,4096]{2,1,0:T(8,128)(2,1)}, u32[]{:S(2)}) copy-start(bf16[2,96,4096]{2,1,0:T(8,128)(2,1)} %param.13) | copy-start | bytes 4718596
  6.5 114.7 %all-gather.4.cloned.1.call-start = ((), (), s32[]{:S(2)}) async-start(), calls=%async_computation.5 | async-start | bytes 2162688 | tf_op jit(solution)/shard_map/all_gather | solution.py:32
  50.6 390.4 %reduce-scatter.3.cloned.1.call-start = ((), (), s32[]{:S(2)}) async-start(), calls=%async_computation.3 | async-start | bytes 13369344 | tf_op jit(solution)/shard_map/reduce_scatter | solution.py:60
  337.3 218.9 %reduce-scatter.5.cloned.1.call-start = ((), (), s32[]{:S(2)}) async-start(), calls=%async_computation.4 | async-start | bytes 2162688 | tf_op jit(solution)/shard_map/reduce_scatter | solution.py:64
Sparse Core Ops, SparseCore 0:
  50.7 70.4 all-gather.3
  337.5 103.4 reduce-scatter.2
  446.4 109.8 reduce-scatter.4

commit v2 on v0

--- a/solution.py
+++ b/solution.py
@@ -15,7 +15,7 @@
     experts_all = exp_local * groups
     capacity = min(tokens_here, 3 * tokens_here * choices_count // (2 * experts_all))
     widened = hidden_in.astype(jnp.float32)
-    squares = lax.psum(jnp.sum(widened * widened, axis=1), "tensor")
+    squares = jnp.sum(lax.all_gather(jnp.sum(widened * widened, axis=1), "tensor"), axis=0)
     normed = (widened * lax.rsqrt(squares / D + epsilon)[:, None] * norm_gain[None, :]).astype(
         jnp.bfloat16
     )

time: 492 us -> 475 us (0.965)
  the two profiles are of different devices: /device:TPU:18 before, /device:TPU:14 now
where the time goes in v2:
time: 475 us
  waiting for transfers between devices  368 us (77%)
  blocking collectives  56.3 us (12%)
  matrix products  31.7 us (7%)
  between operations  13.2 us (3%)
    reduce_scatter x1, waiting for transfers between devices, body(): lax.psum_scatter(weighted, 'expert', scatter_dimension=0, tiled=False)  111 us
    all_gather x1, waiting for transfers between devices, body(): piece = lax.all_gather(rows, 'tensor', axis=2, tiled=True)  110 us
    reduce_scatter x1, waiting for transfers between devices, body(): lax.psum_scatter(partials, 'tensor', scatter_dimension=2, tiled=True)  109 us
    all_gather x1, waiting for transfers between devices, body(): tokens_all = lax.all_gather(normed, 'expert', axis=0, tiled=False)  37.3 us
    all_gather x1, blocking collectives, body(): routing = lax.all_gather(routing.T, 'expert', axis=0, tiled=False)  36.2 us
    all_gather x1, blocking collectives, body(): lax.all_gather(jnp.sum(widened * widened, axis=1), 'tensor')  20.1 us
    dot_general x1, matrix products, body(): jnp.einsum('erf,efd->erd', inner, w_down, preferred_element_type=jnp.floa...  15.3 us
  transfers between devices with their start and end apart: 4, of which 4 were waited for; matrix products, arithmetic and copies ran while one was open for 0% of the time, Pallas kernels for 0%

profile of v2, /device:TPU:14, one launch (start us, length us, event | category | flops | bytes accessed | tf_op | source)
XLA Modules:
  0.0 474.6 jit_solution(1816265366170456552)
XLA Ops:
  6.5 0.0 copy-start
  6.5 0.0 all-gather.9.cloned.1.call-start
  6.5 1.1 fusion.17
  7.6 20.1 %all-gather.3 = f32[16,1,128]{2,1,0:T(1,128)S(1)} all-gather(f32[1,1,128]{2,1,0:T(1,128)S(1)} %bitcast.26), channel_id=3, replica_groups=mesh['expert'=32,'tensor'=16] {'tensor'}, dimensions={0}, use_global_device_ids=true | all-gather | bytes 8704 | tf_op jit(solution)/shard_map/all_gather | solution.py:18
  27.8 1.6 fusion.19
  29.3 0.0 all-gather.9.cloned.1.call-update
  29.3 0.0 all-gather.7.cloned.1.call-start
  29.4 0.7 convert_element_type.31
  30.1 0.7 maximum_bitcast_fusion
  30.8 36.2 %all-gather = f32[512,128]{1,0:T(8,128)S(1)} all-gather(f32[16,128]{1,0:T(8,128)S(1)} %maximum_bitcast_fusion), channel_id=2, replica_groups=mesh['expert'=32,'tensor'=16] {'expert'}, dimensions={0}, use_global_device_ids=true | all-gather | bytes 270336 | tf_op jit(solution)/shard_map/all_gather | solution.py:23
  67.0 0.2 compare_reduce_fusion
  67.2 0.1 fusion.21
  67.4 37.3 %all-gather.9.cloned.1.call-done = bf16[4096,256]{1,0:T(8,128)(2,1)} async-done(((bf16[128,256]{1,0:T(8,128)(2,1)}), bf16[4096,256]{1,0:T(8,128)(2,1)}) %all-gather.9.cloned.1.call-update) | async-done | bytes 2097168 | tf_op jit(solution)/shard_map/all_gather | solution.py:24
  104.6 2.0 fusion
  106.7 1.0 copy.21
  107.6 0.0 all-gather.7.cloned.1.call-update
  107.7 0.0 reduce-scatter.3.cloned.1.call-start
  107.7 110.4 %all-gather.7.cloned.1.call-done = bf16[2,768,4096]{2,1,0:T(8,128)(2,1)} async-done(((bf16[2,768,256]{2,1,0:T(8,128)(2,1)}), bf16[2,768,4096]{2,1,0:T(8,128)(2,1)}) %all-gather.7.cloned.1.call-update) | async-done | bytes 12582928 | tf_op jit(solution)/shard_map/all_gather | solution.py:45
  218.2 9.0 %fusion.26 = f32[2,768,96]{1,2,0:T(8,128)S(1)} fusion(bf16[2,768,4096]{2,1,0:T(8,128)(2,1)} %all-gather.7.cloned.1.call-done, bf16[2,96,4096]{2,1,0:T(8,128)(2,1)} %param.11), kind=kOutput, calls=%fused_computation.36 | convolution fusion | flops 1207959552 | bytes 14745600 | tf_op jit(solution)/shard_map/erd,efd->erf/dot_general | solution.py:46
  227.1 0.0 copy-done
  227.1 15.3 %convolution_convert_fusion = bf16[2,768,4096]{2,1,0:T(8,128)(2,1)} fusion(bf16[2,96,4096]{2,1,0:T(8,128)(2,1)S(1)} %copy-done, bf16[2,768,4096]{2,1,0:T(8,128)(2,1)} %all-gather.7.cloned.1.call-done, bf16[2,96,4096]{2,1,0:T(8,128)(2,1)} %param.12, f32[2,768,96]{1,2,0:T(8,128)S(1)} %fusion.26), kind=kOutput, calls=%fused_computation | convolution fusion | flops 2423095296 | bytes 28901376 | tf_op jit(solution)/shard_map/erf,efd->erd/dot_general | solution.py:49
  242.4 0.0 reduce-scatter.3.cloned.1.call-update
  242.5 0.0 reduce-scatter.5.cloned.1.call-start
  242.5 0.2 fusion.16
  242.7 108.8 %reduce-scatter.3.cloned.1.call-done = bf16[2,768,256]{2,1,0:T(8,128)(2,1)} async-done(((bf16[2,768,4096]{2,1,0:T(8,128)(2,1)}), bf16[2,768,256]{2,1,0:T(8,128)(2,1)}) %reduce-scatter.3.cloned.1.call-update) | async-done | bytes 786448 | tf_op jit(solution)/shard_map/reduce_scatter | solution.py:52
  351.5 5.3 %multiply_reduce_fusion = bf16[32,128,256]{2,1,0:T(8,128)(2,1)} fusion(f32[32,2,128]{2,1,0:T(2,128)S(1)} %fusion.16, bf16[2,32,24,256]{3,2,1,0:T(8,128)(2,1)} %bitcast.27, f32[32,2,128]{2,1,0:T(2,128)S(1)} %copy.20, pred[32,2,128]{2,1,0:T(4,128)(4,1)S(1)} %compare_reduce_fusion), kind=kOutput, calls=%fused_computation.1 | convolution fusion | flops 104202240 | bytes 2957312 | tf_op jit(solution)/shard_map/bjst,jbsd->bjtd/dot_general | solution.py:54
  356.8 0.0 reduce-scatter.5.cloned.1.call-update
  356.9 111.2 %reduce-scatter.5.cloned.1.call-done = bf16[1,128,256]{2,1,0:T(8,128)(2,1)} async-done(((bf16[32,128,256]{2,1,0:T(8,128)(2,1)}), bf16[1,128,256]{2,1,0:T(8,128)(2,1)}) %reduce-scatter.5.cloned.1.call-update) | async-done | bytes 65552 | tf_op jit(solution)/shard_map/reduce_scatter | solution.py:56
  (5 shorter events, 0.1 us)
Async XLA Ops:
  6.5 220.6 %copy-start = (bf16[2,96,4096]{2,1,0:T(8,128)(2,1)S(1)}, bf16[2,96,4096]{2,1,0:T(8,128)(2,1)}, u32[]{:S(2)}) copy-start(bf16[2,96,4096]{2,1,0:T(8,128)(2,1)} %param.13) | copy-start | bytes 4718596
  6.5 98.1 %all-gather.9.cloned.1.call-start = ((), (), s32[]{:S(2)}) async-start(), calls=%async_computation.5 | async-start | bytes 2162688 | tf_op jit(solution)/shard_map/all_gather | solution.py:24
  29.3 188.8 %all-gather.7.cloned.1.call-start = ((), (), s32[]{:S(2)}) async-start(), calls=%async_computation.2 | async-start | bytes 13369344 | tf_op jit(solution)/shard_map/all_gather | solution.py:45
  107.7 243.9 %reduce-scatter.3.cloned.1.call-start = ((), (), s32[]{:S(2)}) async-start(), calls=%async_computation.3 | async-start | bytes 13369344 | tf_op jit(solution)/shard_map/reduce_scatter | solution.py:52
  242.5 225.6 %reduce-scatter.5.cloned.1.call-start = ((), (), s32[]{:S(2)}) async-start(), calls=%async_computation.4 | async-start | bytes 2162688 | tf_op jit(solution)/shard_map/reduce_scatter | solution.py:56
Sparse Core Ops, SparseCore 0:
  29.5 75.1 all-gather.8
  107.8 110.3 all-gather.6
  242.6 108.8 reduce-scatter.2
  357.0 111.0 reduce-scatter.4
